TPU v7x, 128 devices: a whole 4x4x4 slice. The times are simulated.
128 devices in a mesh: row: 16 (over x, y), col: 8 (over z, core).
Axes of the slice: x: 4, y: 4, z: 4, core: 2. Of those that a mesh axis runs over, the one named last changes fastest.
Arguments:
- features: bfloat16 [49152, 256], P(('row', 'col')), may hold values from -6 to 6
- weight: bfloat16 [256, 256], replicated, may hold values from -0.375 to 0.375
- out_bias: float32 [256], replicated, may hold values from -3 to 3
- cotangent: bfloat16 [49152, 256], P(('row', 'col')), may hold values from -6 to 6
- adj_tiles: bfloat16 [16, 8, 24, 16, 128, 128], P('row', 'col'), may hold values from -0.125 to 0.125
- tile_cols: int32 [16, 8, 24, 16], P('row', 'col'), may hold values from 0 to 47, as said below
- tile_counts: int32 [16, 8, 24], P('row', 'col'), may hold values from 1 to 16, as said below
Outputs:
- activated: bfloat16 [49152, 256], P(('row', 'col'))
- grad_features: bfloat16 [49152, 256], P(('row', 'col'))
- grad_weight: float32 [256, 256], replicated
- grad_bias: float32 [256], replicated
Inputs may be any that keep to these rules, and one draw needn't show every extreme that they name: `tile_cols`: within a tile row of a block the 16 column numbers are distinct. `tile_counts`: every block has a tile row whose 16 slots are all live.
All inputs are finite; a program needn't handle non-finite values.
Results may differ from a plain program's by a relative error of at most 0.02.
Values may be sent and summed in bfloat16 or wider, within the bound.
No kernel may reach another device: no remote copies, remote signals or barrier semaphores. Data moves between devices by JAX's collectives and lax.ppermute only.
A program may use at most 192 MiB of HBM per device.

v0:
```python
import jax
import jax.numpy as jnp
from jax import lax
from jax.sharding import PartitionSpec as P


def tile_products(blocks, columns, live_mask, panel_tiles):
    accumulated = jnp.zeros((blocks.shape[0], blocks.shape[2], panel_tiles.shape[2]), jnp.float32)
    for position in range(blocks.shape[1]):
        picked = jnp.take(panel_tiles, columns[:, position], axis=0)
        product = jnp.einsum(
            "tab,tbf->taf", blocks[:, position], picked, preferred_element_type=jnp.float32
        )
        accumulated = accumulated + product * live_mask[:, position, None, None]
    return accumulated


def shards(features, weight, out_bias, cotangent, adj_tiles, tile_cols, tile_counts):
    node_dev = features.shape[0]
    feat_width = features.shape[1]
    tile_size = adj_tiles.shape[-1]
    slot_count = adj_tiles.shape[3]
    tile_rows = adj_tiles.shape[2]
    row_count = lax.axis_size("row")
    col_count = lax.axis_size("col")
    column_tiles = row_count * node_dev // tile_size
    blocks = adj_tiles.reshape(tile_rows, slot_count, tile_size, tile_size)
    columns = tile_cols.reshape(tile_rows, slot_count)
    slot_iota = lax.broadcasted_iota(jnp.int32, (tile_rows, slot_count), 1)
    live_mask = (slot_iota < tile_counts.reshape(tile_rows, 1)).astype(jnp.float32)
    gathered = jnp.dot(
        lax.all_gather(features, "row", axis=0, tiled=True),
        weight,
        preferred_element_type=jnp.float32,
    ).astype(jnp.bfloat16)
    panel_tiles = gathered.reshape(column_tiles, tile_size, feat_width)
    accumulated = tile_products(blocks, columns, live_mask, panel_tiles)
    rounded = accumulated.astype(jnp.bfloat16).astype(jnp.float32)
    summed = lax.psum_scatter(
        rounded.reshape(tile_rows * tile_size, feat_width).astype(jnp.bfloat16),
        "col",
        scatter_dimension=0,
        tiled=True,
    ).astype(jnp.float32)
    preact = summed + out_bias
    sigmoid_val = jax.nn.sigmoid(preact)
    activated = (preact * sigmoid_val).astype(jnp.bfloat16)
    grad_preact = (
        cotangent.astype(jnp.float32) * sigmoid_val * (1.0 + preact * (1.0 - sigmoid_val))
    ).astype(jnp.bfloat16)
    initial = jnp.zeros((column_tiles, tile_size, feat_width), jnp.float32)
    running = initial
    shard_rows = lax.all_gather(grad_preact, "col", axis=0, tiled=True)
    row_tiles = shard_rows.shape[0] // tile_size
    grad_tiles = shard_rows.reshape(row_tiles, tile_size, feat_width)
    for position in range(slot_count):
        product = jnp.einsum(
            "tab,taf->tbf", blocks[:, position], grad_tiles, preferred_element_type=jnp.float32
        )
        running = running.at[columns[:, position]].add(product * live_mask[:, position, None, None])
    back_rounded = running.astype(jnp.bfloat16).astype(jnp.float32)
    grad_projected = lax.psum_scatter(
        back_rounded.reshape(column_tiles * tile_size, feat_width).astype(jnp.bfloat16),
        "row",
        scatter_dimension=0,
        tiled=True,
    )
    grad_features = lax.dot_general(
        grad_projected, weight, (((1,), (1,)), ((), ())), preferred_element_type=jnp.float32
    ).astype(jnp.bfloat16)
    weight_part = lax.dot_general(
        features, grad_projected, (((0,), (0,)), ((), ())), preferred_element_type=jnp.float32
    )
    bias_part = jnp.sum(grad_preact.astype(jnp.float32), axis=0)
    scale_factor = (node_dev * row_count * col_count) ** (-0.5)
    weight_total, bias_total = lax.psum((weight_part, bias_part), ("row", "col"))
    return (activated, grad_features, weight_total * scale_factor, bias_total * scale_factor)


def solution(mesh):
    in_specs = (
        P(("row", "col"), None),
        P(),
        P(),
        P(("row", "col"), None),
        P("row", "col", None, None, None, None),
        P("row", "col", None, None),
        P("row", "col", None),
    )
    out_specs = (P(("row", "col"), None), P(("row", "col"), None), P(), P())
    return jax.shard_map(shards, mesh=mesh, in_specs=in_specs, out_specs=out_specs, check_vma=False)
```

profile of v0, /device:TPU:1, one launch (start us, length us, event | category | flops | bytes accessed | tf_op | source)
XLA Modules:
  0.0 643.4 jit_solution(12031219204387796156)
XLA Ops:
  8.0 11.9 %copy.96 = bf16[1,1,24,16,128,128]{5,4,2,3,1,0:T(8,128)(2,1)} copy(bf16[1,1,24,16,128,128]{5,4,3,2,1,0:T(8,128)(2,1)} %param.13) | data formatting | bytes 25165824 | tf_op args[4]
  20.0 40.4 %all-gather.3.cloned.1.call-done = bf16[6144,256]{1,0:T(8,128)(2,1)} async-done(((bf16[384,256]{1,0:T(8,128)(2,1)}), bf16[6144,256]{1,0:T(8,128)(2,1)}) %all-gather.3.cloned.1.call-update) | async-done | bytes 3145744 | tf_op jit(solution)/shard_map/all_gather | solution.py:32
  133.4 17.8 %bitcast_convert_fusion = bf16[24,128,256]{2,1,0:T(8,128)(2,1)} fusion(f32[24,256,128]{1,2,0:T(8,128)} %fusion.1, f32[24,256,128]{1,2,0:T(8,128)} %fusion.3, f32[24,256,128]{1,2,0:T(8,128)} %fusion.5, f32[24,256,128]{1,2,0:T(8,128)} %fusion.7, f32[24,256,128]{1,2,0:T(8,128)} %fusion.9, f32[24,256,128]{1,2,0:T(8,128)S(1)} %fusion.11, ...), kind=kOutput, calls=%fused_computation.34 | convolution fusion | flops 227278848 | bytes 51119640 | tf_op jit(solution)/shard_map/tab,tbf->taf/dot_general | solution.py:11
  151.3 29.8 %reduce-scatter.3.cloned.1.call-done = bf16[384,256]{1,0:T(8,128)(2,1)} async-done(((bf16[3072,256]{1,0:T(8,128)(2,1)}), bf16[384,256]{1,0:T(8,128)(2,1)}) %reduce-scatter.3.cloned.1.call-update) | async-done | bytes 196624 | tf_op jit(solution)/shard_map/reduce_scatter | solution.py:39
  183.1 26.9 %all-gather.5.cloned.1.call-done = bf16[3072,256]{1,0:T(8,128)(2,1)} async-done(((bf16[384,256]{1,0:T(8,128)(2,1)}), bf16[3072,256]{1,0:T(8,128)(2,1)}) %all-gather.5.cloned.1.call-update) | async-done | bytes 1572880 | tf_op jit(solution)/shard_map/all_gather | solution.py:53
  256.1 10.0 %scatter_fusion = f32[48,128,256]{2,1,0:T(8,128)} fusion(f32[48,128,256]{2,1,0:T(8,128)} %broadcast_in_dim.11, s32[24]{0:T(128)S(1)} %get-tuple-element.49, f32[24,128,256]{2,1,0:T(8,128)} %multiply_bitcast_fusion.15), kind=kCustom, calls=%fused_computation.16 | custom fusion | flops 786432 | bytes 9437280 | tf_op jit(solution)/shard_map/scatter-add | solution.py:60
  266.1 9.3 %scatter_fusion.1 = f32[48,128,256]{2,1,0:T(8,128)} fusion(f32[48,128,256]{2,1,0:T(8,128)} %scatter_fusion, s32[24]{0:T(128)S(1)} %get-tuple-element.50, f32[24,128,256]{2,1,0:T(8,128)} %multiply_bitcast_fusion.14), kind=kCustom, calls=%fused_computation.17 | custom fusion | flops 786432 | bytes 9437280 | tf_op jit(solution)/shard_map/scatter-add | solution.py:60
  275.4 9.3 %scatter_fusion.2 = f32[48,128,256]{2,1,0:T(8,128)} fusion(f32[48,128,256]{2,1,0:T(8,128)} %scatter_fusion.1, s32[24]{0:T(128)S(1)} %get-tuple-element.51, f32[24,128,256]{2,1,0:T(8,128)} %multiply_bitcast_fusion.13), kind=kCustom, calls=%fused_computation.18 | custom fusion | flops 786432 | bytes 9437280 | tf_op jit(solution)/shard_map/scatter-add | solution.py:60
  284.7 9.4 %scatter_fusion.3 = f32[48,128,256]{2,1,0:T(8,128)} fusion(f32[48,128,256]{2,1,0:T(8,128)} %scatter_fusion.2, s32[24]{0:T(128)S(1)} %get-tuple-element.52, f32[24,128,256]{2,1,0:T(8,128)} %multiply_bitcast_fusion.12), kind=kCustom, calls=%fused_computation.19 | custom fusion | flops 786432 | bytes 9437280 | tf_op jit(solution)/shard_map/scatter-add | solution.py:60
  294.1 9.3 %scatter_fusion.4 = f32[48,128,256]{2,1,0:T(8,128)} fusion(f32[48,128,256]{2,1,0:T(8,128)} %scatter_fusion.3, s32[24]{0:T(128)S(1)} %get-tuple-element.53, f32[24,128,256]{2,1,0:T(8,128)} %multiply_bitcast_fusion.11), kind=kCustom, calls=%fused_computation.20 | custom fusion | flops 786432 | bytes 9437280 | tf_op jit(solution)/shard_map/scatter-add | solution.py:60
  303.4 9.4 %scatter_fusion.5 = f32[48,128,256]{2,1,0:T(8,128)} fusion(f32[48,128,256]{2,1,0:T(8,128)} %scatter_fusion.4, s32[24]{0:T(128)S(1)} %get-tuple-element.54, f32[24,128,256]{2,1,0:T(8,128)} %multiply_bitcast_fusion.10), kind=kCustom, calls=%fused_computation.21 | custom fusion | flops 786432 | bytes 9437280 | tf_op jit(solution)/shard_map/scatter-add | solution.py:60
  312.8 9.5 %scatter_fusion.6 = f32[48,128,256]{2,1,0:T(8,128)} fusion(f32[48,128,256]{2,1,0:T(8,128)} %scatter_fusion.5, s32[24]{0:T(128)S(1)} %get-tuple-element.55, f32[24,128,256]{2,1,0:T(8,128)} %multiply_bitcast_fusion.9), kind=kCustom, calls=%fused_computation.22 | custom fusion | flops 786432 | bytes 9437280 | tf_op jit(solution)/shard_map/scatter-add | solution.py:60
  322.3 9.4 %scatter_fusion.7 = f32[48,128,256]{2,1,0:T(8,128)} fusion(f32[48,128,256]{2,1,0:T(8,128)} %scatter_fusion.6, s32[24]{0:T(128)S(1)} %get-tuple-element.56, f32[24,128,256]{2,1,0:T(8,128)} %multiply_bitcast_fusion.8), kind=kCustom, calls=%fused_computation.23 | custom fusion | flops 786432 | bytes 9437280 | tf_op jit(solution)/shard_map/scatter-add | solution.py:60
  331.8 9.3 %scatter_fusion.8 = f32[48,128,256]{2,1,0:T(8,128)} fusion(f32[48,128,256]{2,1,0:T(8,128)} %scatter_fusion.7, s32[24]{0:T(128)S(1)} %get-tuple-element.57, f32[24,128,256]{2,1,0:T(8,128)} %multiply_bitcast_fusion.7), kind=kCustom, calls=%fused_computation.24 | custom fusion | flops 786432 | bytes 9437280 | tf_op jit(solution)/shard_map/scatter-add | solution.py:60
  341.1 9.6 %scatter_fusion.9 = f32[48,128,256]{2,1,0:T(8,128)} fusion(f32[48,128,256]{2,1,0:T(8,128)} %scatter_fusion.8, s32[24]{0:T(128)S(1)} %get-tuple-element.58, f32[24,128,256]{2,1,0:T(8,128)} %multiply_bitcast_fusion.6), kind=kCustom, calls=%fused_computation.25 | custom fusion | flops 786432 | bytes 9437280 | tf_op jit(solution)/shard_map/scatter-add | solution.py:60
  350.6 9.4 %scatter_fusion.10 = f32[48,128,256]{2,1,0:T(8,128)} fusion(f32[48,128,256]{2,1,0:T(8,128)} %scatter_fusion.9, s32[24]{0:T(128)S(1)} %get-tuple-element.59, f32[24,128,256]{2,1,0:T(8,128)} %multiply_bitcast_fusion.5), kind=kCustom, calls=%fused_computation.26 | custom fusion | flops 786432 | bytes 9437280 | tf_op jit(solution)/shard_map/scatter-add | solution.py:60
  360.0 9.4 %scatter_fusion.11 = f32[48,128,256]{2,1,0:T(8,128)} fusion(f32[48,128,256]{2,1,0:T(8,128)} %scatter_fusion.10, s32[24]{0:T(128)S(1)} %get-tuple-element.60, f32[24,128,256]{2,1,0:T(8,128)} %multiply_bitcast_fusion.4), kind=kCustom, calls=%fused_computation.27 | custom fusion | flops 786432 | bytes 9437280 | tf_op jit(solution)/shard_map/scatter-add | solution.py:60
  369.5 9.3 %scatter_fusion.12 = f32[48,128,256]{2,1,0:T(8,128)} fusion(f32[48,128,256]{2,1,0:T(8,128)} %scatter_fusion.11, s32[24]{0:T(128)S(1)} %get-tuple-element.61, f32[24,128,256]{2,1,0:T(8,128)} %multiply_bitcast_fusion.3), kind=kCustom, calls=%fused_computation.28 | custom fusion | flops 786432 | bytes 9437280 | tf_op jit(solution)/shard_map/scatter-add | solution.py:60
  378.8 9.5 %scatter_fusion.13 = f32[48,128,256]{2,1,0:T(8,128)} fusion(f32[48,128,256]{2,1,0:T(8,128)} %scatter_fusion.12, s32[24]{0:T(128)S(1)} %get-tuple-element.62, f32[24,128,256]{2,1,0:T(8,128)} %multiply_bitcast_fusion.2), kind=kCustom, calls=%fused_computation.29 | custom fusion | flops 786432 | bytes 9437280 | tf_op jit(solution)/shard_map/scatter-add | solution.py:60
  388.3 9.4 %scatter_fusion.14 = f32[48,128,256]{2,1,0:T(8,128)} fusion(f32[48,128,256]{2,1,0:T(8,128)} %scatter_fusion.13, s32[24]{0:T(128)S(1)} %get-tuple-element.63, f32[24,128,256]{2,1,0:T(8,128)} %multiply_bitcast_fusion.1), kind=kCustom, calls=%fused_computation.30 | custom fusion | flops 786432 | bytes 9437280 | tf_op jit(solution)/shard_map/scatter-add | solution.py:60
  397.7 8.4 %scatter_fusion.15 = f32[48,128,256]{2,1,0:T(8,128)} fusion(f32[48,128,256]{2,1,0:T(8,128)} %scatter_fusion.14, s32[24]{0:T(128)S(1)} %get-tuple-element.48, f32[24,128,256]{2,1,0:T(8,128)S(1)} %multiply_bitcast_fusion), kind=kCustom, calls=%fused_computation.31 | custom fusion | flops 786432 | bytes 9437280 | tf_op jit(solution)/shard_map/scatter-add | solution.py:60
  411.1 64.7 %psum.15 = f32[256]{0:T(256)S(1)} all-reduce(f32[256]{0:T(256)S(1)} %get-tuple-element.13), channel_id=1, replica_groups=mesh['row'=16,'col'=8] {'row','col'}, use_global_device_ids=true, to_apply=%region_20.22 | all-reduce | flops 256 | bytes 2048 | tf_op jit(solution)/shard_map/psum | solution.py:76
  476.4 9.1 %reduce-scatter.5.cloned.1.call-done = bf16[384,256]{1,0:T(8,128)(2,1)} async-done(((bf16[6144,256]{1,0:T(8,128)(2,1)}), bf16[384,256]{1,0:T(8,128)(2,1)}) %reduce-scatter.5.cloned.1.call-update) | async-done | bytes 196624 | tf_op jit(solution)/shard_map/reduce_scatter | solution.py:62
  489.3 145.6 %all-reduce.2.cloned.1.call-done = f32[256,256]{0,1:T(8,128)} async-done(((f32[256,256]{0,1:T(8,128)}), f32[256,256]{0,1:T(8,128)}) %all-reduce.2.cloned.1.call-update) | async-done | bytes 262160 | tf_op jit(solution)/shard_map/psum | solution.py:76
  (134 shorter events, 132.9 us)
Async XLA Ops:
  7.2 53.3 %copy-start = (bf16[256,256]{1,0:T(8,128)(2,1)S(1)}, bf16[256,256]{1,0:T(8,128)(2,1)}, u32[]{:S(2)}) copy-start(bf16[256,256]{1,0:T(8,128)(2,1)} %param.10) | copy-start | bytes 393220
  7.2 53.2 %all-gather.3.cloned.1.call-start = ((), (), s32[]{:S(2)}) async-start(), calls=%async_computation.2 | async-start | bytes 3342336 | tf_op jit(solution)/shard_map/all_gather | solution.py:32
  7.9 11.9 %copy-start.18 = (s32[1,1,24,16]{2,3,1,0:T(8,128)S(1)}, s32[1,1,24,16]{2,3,1,0:T(8,128)}, u32[]{:S(2)}) copy-start(s32[1,1,24,16]{2,3,1,0:T(8,128)} %param.14) | copy-start | bytes 4612
  7.9 12.1 %copy-start.20 = (s32[1,1,24]{2,1,0:T(1,128)S(1)}, s32[1,1,24]{2,1,0:T(1,128)}, u32[]{:S(2)}) copy-start(s32[1,1,24]{2,1,0:T(1,128)} %param.15) | copy-start | bytes 292
  7.9 173.2 %reduce-scatter.3.cloned.1.call-start = ((), (), s32[]{:S(2)}) async-start(), calls=%async_computation.3 | async-start | bytes 1769472 | tf_op jit(solution)/shard_map/reduce_scatter | solution.py:39
  93.1 2.5 copy-start.15
  93.1 16.8 %slice-start = ((s8[12582912]{0:T(1024)(128)(4,1)}), s8[4194304]{0:T(1024)(128)(4,1)S(1)}, s32[]{:S(2)}) async-start(s8[12582912]{0:T(1024)(128)(4,1)} %bitcast.286), calls=%async_computation.7 | async-start | bytes 8388608
  95.5 3.6 copy-start.13
  95.6 14.4 %slice-start.1 = ((s8[12582912]{0:T(1024)(128)(4,1)}), s8[4194304]{0:T(1024)(128)(4,1)S(1)}, s32[]{:S(2)}) async-start(s8[12582912]{0:T(1024)(128)(4,1)} %bitcast.286), calls=%async_computation.8 | async-start | bytes 8388608
  99.2 3.6 copy-start.14
  102.7 3.6 copy-start.11
  102.7 7.2 %slice-start.2 = ((s8[12582912]{0:T(1024)(128)(4,1)}), s8[4194304]{0:T(1024)(128)(4,1)S(1)}, s32[]{:S(2)}) async-start(s8[12582912]{0:T(1024)(128)(4,1)} %bitcast.286), calls=%async_computation.9 | async-start | bytes 8388608
  106.4 3.6 copy-start.12
  128.7 2.5 copy-start.2
  133.4 47.7 %copy-start.17 = (bf16[384,256]{1,0:T(8,128)(2,1)S(1)}, bf16[384,256]{1,0:T(8,128)(2,1)}, u32[]{:S(2)}) copy-start(bf16[384,256]{1,0:T(8,128)(2,1)} %param.12) | copy-start | bytes 589828
  133.4 47.7 %copy-start.19 = (f32[256]{0:T(256)S(1)}, f32[256]{0:T(256)}, u32[]{:S(2)}) copy-start(f32[256]{0:T(256)} %param.11) | copy-start | bytes 3076
  151.3 58.8 %all-gather.5.cloned.1.call-start = ((), (), s32[]{:S(2)}) async-start(), calls=%async_computation.4 | async-start | bytes 1769472 | tf_op jit(solution)/shard_map/all_gather | solution.py:53
  183.0 302.5 %reduce-scatter.5.cloned.1.call-start = ((), (), s32[]{:S(2)}) async-start(), calls=%async_computation.5 | async-start | bytes 3342336 | tf_op jit(solution)/shard_map/reduce_scatter | solution.py:62
  210.1 4.2 copy-start.1
  210.1 18.3 %slice-start.3 = ((s8[12582912]{0:T(1024)(128)(4,1)}), s8[4194304]{0:T(1024)(128)(4,1)S(1)}, s32[]{:S(2)}) async-start(s8[12582912]{0:T(1024)(128)(4,1)} %bitcast.298), calls=%async_computation.10 | async-start | bytes 8388608
  214.2 14.1 %slice-start.4 = ((s8[12582912]{0:T(1024)(128)(4,1)}), s8[4194304]{0:T(1024)(128)(4,1)S(1)}, s32[]{:S(2)}) async-start(s8[12582912]{0:T(1024)(128)(4,1)} %bitcast.298), calls=%async_computation.11 | async-start | bytes 8388608
  221.2 7.1 %slice-start.5 = ((s8[12582912]{0:T(1024)(128)(4,1)}), s8[4194304]{0:T(1024)(128)(4,1)S(1)}, s32[]{:S(2)}) async-start(s8[12582912]{0:T(1024)(128)(4,1)} %bitcast.298), calls=%async_computation.12 | async-start | bytes 8388608
  411.0 74.5 %copy-start.16 = (bf16[384,256]{1,0:T(8,128)(2,1)S(1)}, bf16[384,256]{1,0:T(8,128)(2,1)}, u32[]{:S(2)}) copy-start(bf16[384,256]{1,0:T(8,128)(2,1)} %param.9) | copy-start | bytes 589828
  411.1 223.8 %all-reduce.2.cloned.1.call-start = ((), (), s32[]{:S(2)}) async-start(), calls=%async_computation.6 | async-start | bytes 524288 | tf_op jit(solution)/shard_map/psum | solution.py:76
  (8 other events, 18.8 us)
Sparse Core Ops, SparseCore 0:
  10.2 50.2 all-gather.2
  151.4 29.7 reduce-scatter.2
  183.4 26.6 all-gather.4
  411.2 74.3 reduce-scatter.4
  490.7 144.1 all-reduce.1
where the time goes:
time: 653 us; the launch traced here: 643 us
  waiting for transfers between devices  253 us (39%)
  other arithmetic  158 us (24%)
  matrix products  107 us (16%)
  blocking collectives  64.7 us (10%)
  local copies, waits for them, and re-layouts  46 us (7%)
  between operations  14.2 us (2%)
    scatter-add x16, other arithmetic, shards(): running.at[columns[:, position]]  150 us
    psum x1, waiting for transfers between devices, shards(): lax.psum((weight_part, bias_part), ('row', 'col'))  146 us
    psum x1, blocking collectives, shards(): lax.psum((weight_part, bias_part), ('row', 'col'))  64.7 us
    dot_general x16, matrix products, tile_products(): jnp.einsum('tab,tbf->taf', blocks[:, position], picked, preferred_element...  58 us
    dot_general x16, matrix products, shards(): jnp.einsum('tab,taf->tbf', blocks[:, position], grad_tiles, preferred_ele...  42.6 us
    all_gather x1, waiting for transfers between devices, shards(): lax.all_gather(features, 'row', axis=0, tiled=True)  40.4 us
    reduce_scatter x1, waiting for transfers between devices, shards(): lax.psum_scatter(rounded.reshape(tile_rows * tile_size, feat_width).astyp...  29.8 us
    gather x16, local copies, waits for them, and re-layouts, tile_products(): picked = jnp.take(panel_tiles, columns[:, position], axis=0)  29.8 us
  transfers between devices with their start and end apart: 5, of which 5 were waited for; matrix products, arithmetic and copies ran while one was open for 2% of the time, Pallas kernels for 0%

commit v1 on v0

--- a/solution.py
+++ b/solution.py
@@ -73,7 +73,7 @@
     )
     bias_part = jnp.sum(grad_preact.astype(jnp.float32), axis=0)
     scale_factor = (node_dev * row_count * col_count) ** (-0.5)
-    weight_total, bias_total = lax.psum((weight_part, bias_part), ("row", "col"))
+    weight_total, bias_total = lax.psum(lax.psum((weight_part, bias_part), "col"), "row")
     return (activated, grad_features, weight_total * scale_factor, bias_total * scale_factor)
 
 

time: 653 us -> 655 us (level)
  blocking collectives: 64.7 us -> 45.4 us
  waiting for transfers between devices: 253 us -> 271 us
    reduce_scatter x1, waiting for transfers between devices: 9.14 us -> 74.2 us  [shards(): lax.psum_scatter(back_rounded.reshape(column_tiles * tile_size, feat_widt...]
    psum x1 -> x2, waiting for transfers between devices: 146 us -> 99.2 us  [the longest x1 84.4 us: shards(): lax.psum(lax.psum((weight_part, bias_part), 'col'), 'row')]
    psum x1 -> x2, blocking collectives: 64.7 us -> 45.4 us  [the longest x1 31.2 us: shards(): lax.psum(lax.psum((weight_part, bias_part), 'col'), 'row')]
  transfers between devices with their start and end apart: 5 -> 6, of which waited for: 5 -> 6; matrix products, arithmetic and copies ran while one was open for 2% -> 2% of each run, Pallas kernels for 0% -> 0%
where the time goes in v1:
time: 655 us; the launch traced here: 643 us
  waiting for transfers between devices  271 us (41%)
  other arithmetic  158 us (24%)
  matrix products  107 us (16%)
  local copies, waits for them, and re-layouts  46 us (7%)
  blocking collectives  45.4 us (7%)
  between operations  14.8 us (2%)
    scatter-add x16, other arithmetic, shards(): running.at[columns[:, position]]  150 us
    psum x1, waiting for transfers between devices, shards(): lax.psum(lax.psum((weight_part, bias_part), 'col'), 'row')  84.4 us
    reduce_scatter x1, waiting for transfers between devices, shards(): lax.psum_scatter(back_rounded.reshape(column_tiles * tile_size, feat_widt...  74.2 us
    dot_general x16, matrix products, tile_products(): jnp.einsum('tab,tbf->taf', blocks[:, position], picked, preferred_element...  58 us
    dot_general x16, matrix products, shards(): jnp.einsum('tab,taf->tbf', blocks[:, position], grad_tiles, preferred_ele...  42.6 us
    all_gather x1, waiting for transfers between devices, shards(): lax.all_gather(features, 'row', axis=0, tiled=True)  40.4 us
    psum x1, blocking collectives, shards(): lax.psum(lax.psum((weight_part, bias_part), 'col'), 'row')  31.2 us
    gather x16, local copies, waits for them, and re-layouts, tile_products(): picked = jnp.take(panel_tiles, columns[:, position], axis=0)  29.8 us
  transfers between devices with their start and end apart: 6, of which 6 were waited for; matrix products, arithmetic and copies ran while one was open for 2% of the time, Pallas kernels for 0%

profile of v1, /device:TPU:1, one launch (start us, length us, event | category | flops | bytes accessed | tf_op | source)
XLA Modules:
  0.0 643.4 jit_solution(12315616212110445543)
XLA Ops:
  8.0 11.9 %copy.96 = bf16[1,1,24,16,128,128]{5,4,2,3,1,0:T(8,128)(2,1)} copy(bf16[1,1,24,16,128,128]{5,4,3,2,1,0:T(8,128)(2,1)} %param.13) | data formatting | bytes 25165824 | tf_op args[4]
  20.0 40.4 %all-gather.3.cloned.1.call-done = bf16[6144,256]{1,0:T(8,128)(2,1)} async-done(((bf16[384,256]{1,0:T(8,128)(2,1)}), bf16[6144,256]{1,0:T(8,128)(2,1)}) %all-gather.3.cloned.1.call-update) | async-done | bytes 3145744 | tf_op jit(solution)/shard_map/all_gather | solution.py:32
  133.4 17.8 %bitcast_convert_fusion = bf16[24,128,256]{2,1,0:T(8,128)(2,1)} fusion(f32[24,256,128]{1,2,0:T(8,128)} %fusion.1, f32[24,256,128]{1,2,0:T(8,128)} %fusion.3, f32[24,256,128]{1,2,0:T(8,128)} %fusion.5, f32[24,256,128]{1,2,0:T(8,128)} %fusion.7, f32[24,256,128]{1,2,0:T(8,128)} %fusion.9, f32[24,256,128]{1,2,0:T(8,128)S(1)} %fusion.11, ...), kind=kOutput, calls=%fused_computation.34 | convolution fusion | flops 227278848 | bytes 51119640 | tf_op jit(solution)/shard_map/tab,tbf->taf/dot_general | solution.py:11
  151.3 29.8 %reduce-scatter.3.cloned.1.call-done = bf16[384,256]{1,0:T(8,128)(2,1)} async-done(((bf16[3072,256]{1,0:T(8,128)(2,1)}), bf16[384,256]{1,0:T(8,128)(2,1)}) %reduce-scatter.3.cloned.1.call-update) | async-done | bytes 196624 | tf_op jit(solution)/shard_map/reduce_scatter | solution.py:39
  183.0 27.0 %all-gather.5.cloned.1.call-done = bf16[3072,256]{1,0:T(8,128)(2,1)} async-done(((bf16[384,256]{1,0:T(8,128)(2,1)}), bf16[3072,256]{1,0:T(8,128)(2,1)}) %all-gather.5.cloned.1.call-update) | async-done | bytes 1572880 | tf_op jit(solution)/shard_map/all_gather | solution.py:53
  256.1 9.8 %scatter_fusion = f32[48,128,256]{2,1,0:T(8,128)} fusion(f32[48,128,256]{2,1,0:T(8,128)} %broadcast_in_dim.11, s32[24]{0:T(128)S(1)} %get-tuple-element.49, f32[24,128,256]{2,1,0:T(8,128)} %multiply_bitcast_fusion.15), kind=kCustom, calls=%fused_computation.16 | custom fusion | flops 786432 | bytes 9437280 | tf_op jit(solution)/shard_map/scatter-add | solution.py:60
  265.9 9.3 %scatter_fusion.1 = f32[48,128,256]{2,1,0:T(8,128)} fusion(f32[48,128,256]{2,1,0:T(8,128)} %scatter_fusion, s32[24]{0:T(128)S(1)} %get-tuple-element.50, f32[24,128,256]{2,1,0:T(8,128)} %multiply_bitcast_fusion.14), kind=kCustom, calls=%fused_computation.17 | custom fusion | flops 786432 | bytes 9437280 | tf_op jit(solution)/shard_map/scatter-add | solution.py:60
  284.5 9.4 %scatter_fusion.3 = f32[48,128,256]{2,1,0:T(8,128)} fusion(f32[48,128,256]{2,1,0:T(8,128)} %scatter_fusion.2, s32[24]{0:T(128)S(1)} %get-tuple-element.52, f32[24,128,256]{2,1,0:T(8,128)} %multiply_bitcast_fusion.12), kind=kCustom, calls=%fused_computation.19 | custom fusion | flops 786432 | bytes 9437280 | tf_op jit(solution)/shard_map/scatter-add | solution.py:60
  293.9 9.3 %scatter_fusion.4 = f32[48,128,256]{2,1,0:T(8,128)} fusion(f32[48,128,256]{2,1,0:T(8,128)} %scatter_fusion.3, s32[24]{0:T(128)S(1)} %get-tuple-element.53, f32[24,128,256]{2,1,0:T(8,128)} %multiply_bitcast_fusion.11), kind=kCustom, calls=%fused_computation.20 | custom fusion | flops 786432 | bytes 9437280 | tf_op jit(solution)/shard_map/scatter-add | solution.py:60
  303.2 9.4 %scatter_fusion.5 = f32[48,128,256]{2,1,0:T(8,128)} fusion(f32[48,128,256]{2,1,0:T(8,128)} %scatter_fusion.4, s32[24]{0:T(128)S(1)} %get-tuple-element.54, f32[24,128,256]{2,1,0:T(8,128)} %multiply_bitcast_fusion.10), kind=kCustom, calls=%fused_computation.21 | custom fusion | flops 786432 | bytes 9437280 | tf_op jit(solution)/shard_map/scatter-add | solution.py:60
  312.6 9.5 %scatter_fusion.6 = f32[48,128,256]{2,1,0:T(8,128)} fusion(f32[48,128,256]{2,1,0:T(8,128)} %scatter_fusion.5, s32[24]{0:T(128)S(1)} %get-tuple-element.55, f32[24,128,256]{2,1,0:T(8,128)} %multiply_bitcast_fusion.9), kind=kCustom, calls=%fused_computation.22 | custom fusion | flops 786432 | bytes 9437280 | tf_op jit(solution)/shard_map/scatter-add | solution.py:60
  322.1 9.4 %scatter_fusion.7 = f32[48,128,256]{2,1,0:T(8,128)} fusion(f32[48,128,256]{2,1,0:T(8,128)} %scatter_fusion.6, s32[24]{0:T(128)S(1)} %get-tuple-element.56, f32[24,128,256]{2,1,0:T(8,128)} %multiply_bitcast_fusion.8), kind=kCustom, calls=%fused_computation.23 | custom fusion | flops 786432 | bytes 9437280 | tf_op jit(solution)/shard_map/scatter-add | solution.py:60
  331.6 9.3 %scatter_fusion.8 = f32[48,128,256]{2,1,0:T(8,128)} fusion(f32[48,128,256]{2,1,0:T(8,128)} %scatter_fusion.7, s32[24]{0:T(128)S(1)} %get-tuple-element.57, f32[24,128,256]{2,1,0:T(8,128)} %multiply_bitcast_fusion.7), kind=kCustom, calls=%fused_computation.24 | custom fusion | flops 786432 | bytes 9437280 | tf_op jit(solution)/shard_map/scatter-add | solution.py:60
  340.9 9.6 %scatter_fusion.9 = f32[48,128,256]{2,1,0:T(8,128)} fusion(f32[48,128,256]{2,1,0:T(8,128)} %scatter_fusion.8, s32[24]{0:T(128)S(1)} %get-tuple-element.58, f32[24,128,256]{2,1,0:T(8,128)} %multiply_bitcast_fusion.6), kind=kCustom, calls=%fused_computation.25 | custom fusion | flops 786432 | bytes 9437280 | tf_op jit(solution)/shard_map/scatter-add | solution.py:60
  350.5 9.4 %scatter_fusion.10 = f32[48,128,256]{2,1,0:T(8,128)} fusion(f32[48,128,256]{2,1,0:T(8,128)} %scatter_fusion.9, s32[24]{0:T(128)S(1)} %get-tuple-element.59, f32[24,128,256]{2,1,0:T(8,128)} %multiply_bitcast_fusion.5), kind=kCustom, calls=%fused_computation.26 | custom fusion | flops 786432 | bytes 9437280 | tf_op jit(solution)/shard_map/scatter-add | solution.py:60
  359.9 9.4 %scatter_fusion.11 = f32[48,128,256]{2,1,0:T(8,128)} fusion(f32[48,128,256]{2,1,0:T(8,128)} %scatter_fusion.10, s32[24]{0:T(128)S(1)} %get-tuple-element.60, f32[24,128,256]{2,1,0:T(8,128)} %multiply_bitcast_fusion.4), kind=kCustom, calls=%fused_computation.27 | custom fusion | flops 786432 | bytes 9437280 | tf_op jit(solution)/shard_map/scatter-add | solution.py:60
  369.3 9.3 %scatter_fusion.12 = f32[48,128,256]{2,1,0:T(8,128)} fusion(f32[48,128,256]{2,1,0:T(8,128)} %scatter_fusion.11, s32[24]{0:T(128)S(1)} %get-tuple-element.61, f32[24,128,256]{2,1,0:T(8,128)} %multiply_bitcast_fusion.3), kind=kCustom, calls=%fused_computation.28 | custom fusion | flops 786432 | bytes 9437280 | tf_op jit(solution)/shard_map/scatter-add | solution.py:60
  378.7 9.5 %scatter_fusion.13 = f32[48,128,256]{2,1,0:T(8,128)} fusion(f32[48,128,256]{2,1,0:T(8,128)} %scatter_fusion.12, s32[24]{0:T(128)S(1)} %get-tuple-element.62, f32[24,128,256]{2,1,0:T(8,128)} %multiply_bitcast_fusion.2), kind=kCustom, calls=%fused_computation.29 | custom fusion | flops 786432 | bytes 9437280 | tf_op jit(solution)/shard_map/scatter-add | solution.py:60
  388.2 9.4 %scatter_fusion.14 = f32[48,128,256]{2,1,0:T(8,128)} fusion(f32[48,128,256]{2,1,0:T(8,128)} %scatter_fusion.13, s32[24]{0:T(128)S(1)} %get-tuple-element.63, f32[24,128,256]{2,1,0:T(8,128)} %multiply_bitcast_fusion.1), kind=kCustom, calls=%fused_computation.30 | custom fusion | flops 786432 | bytes 9437280 | tf_op jit(solution)/shard_map/scatter-add | solution.py:60
  411.0 74.2 %reduce-scatter.5.cloned.1.call-done = bf16[384,256]{1,0:T(8,128)(2,1)} async-done(((bf16[6144,256]{1,0:T(8,128)(2,1)}), bf16[384,256]{1,0:T(8,128)(2,1)}) %reduce-scatter.5.cloned.1.call-update) | async-done | bytes 196624 | tf_op jit(solution)/shard_map/reduce_scatter | solution.py:62
  487.2 14.3 %psum.30 = f32[256]{0:T(256)S(1)} all-reduce(f32[256]{0:T(256)S(1)} %get-tuple-element.13), channel_id=1, replica_groups=mesh['row'=16,'col'=8] {'col'}, use_global_device_ids=true, to_apply=%region_21.23 | all-reduce | flops 256 | bytes 2048 | tf_op jit(solution)/shard_map/psum | solution.py:76
  501.5 31.2 %psum.31 = f32[256]{0:T(256)S(1)} all-reduce(f32[256]{0:T(256)S(1)} %psum.30), channel_id=1, replica_groups=mesh['row'=16,'col'=8] {'row'}, use_global_device_ids=true, to_apply=%region_22.24 | all-reduce | flops 256 | bytes 2048 | tf_op jit(solution)/shard_map/psum | solution.py:76
  532.6 14.8 %all-reduce.3.cloned.1.call-done = f32[256,256]{0,1:T(8,128)} async-done(((f32[256,256]{0,1:T(8,128)}), f32[256,256]{0,1:T(8,128)}) %all-reduce.3.cloned.1.call-update) | async-done | bytes 262160 | tf_op jit(solution)/shard_map/psum | solution.py:76
  549.9 84.4 %all-reduce.5.cloned.1.call-done = f32[256,256]{0,1:T(8,128)} async-done(((f32[256,256]{0,1:T(8,128)}), f32[256,256]{0,1:T(8,128)}) %all-reduce.5.cloned.1.call-update) | async-done | bytes 262160 | tf_op jit(solution)/shard_map/psum | solution.py:76
  (138 shorter events, 150.7 us)
Async XLA Ops:
  7.2 53.3 %copy-start = (bf16[256,256]{1,0:T(8,128)(2,1)S(1)}, bf16[256,256]{1,0:T(8,128)(2,1)}, u32[]{:S(2)}) copy-start(bf16[256,256]{1,0:T(8,128)(2,1)} %param.10) | copy-start | bytes 393220
  7.2 53.2 %all-gather.3.cloned.1.call-start = ((), (), s32[]{:S(2)}) async-start(), calls=%async_computation.2 | async-start | bytes 3342336 | tf_op jit(solution)/shard_map/all_gather | solution.py:32
  7.9 11.9 %copy-start.18 = (s32[1,1,24,16]{2,3,1,0:T(8,128)S(1)}, s32[1,1,24,16]{2,3,1,0:T(8,128)}, u32[]{:S(2)}) copy-start(s32[1,1,24,16]{2,3,1,0:T(8,128)} %param.14) | copy-start | bytes 4612
  7.9 12.1 %copy-start.20 = (s32[1,1,24]{2,1,0:T(1,128)S(1)}, s32[1,1,24]{2,1,0:T(1,128)}, u32[]{:S(2)}) copy-start(s32[1,1,24]{2,1,0:T(1,128)} %param.15) | copy-start | bytes 292
  7.9 173.1 %reduce-scatter.3.cloned.1.call-start = ((), (), s32[]{:S(2)}) async-start(), calls=%async_computation.3 | async-start | bytes 1769472 | tf_op jit(solution)/shard_map/reduce_scatter | solution.py:39
  93.1 16.8 %slice-start = ((s8[12582912]{0:T(1024)(128)(4,1)}), s8[4194304]{0:T(1024)(128)(4,1)S(1)}, s32[]{:S(2)}) async-start(s8[12582912]{0:T(1024)(128)(4,1)} %bitcast.286), calls=%async_computation.8 | async-start | bytes 8388608
  95.5 3.6 copy-start.13
  95.6 14.4 %slice-start.1 = ((s8[12582912]{0:T(1024)(128)(4,1)}), s8[4194304]{0:T(1024)(128)(4,1)S(1)}, s32[]{:S(2)}) async-start(s8[12582912]{0:T(1024)(128)(4,1)} %bitcast.286), calls=%async_computation.9 | async-start | bytes 8388608
  99.2 3.6 copy-start.14
  102.7 3.6 copy-start.11
  102.7 7.2 %slice-start.2 = ((s8[12582912]{0:T(1024)(128)(4,1)}), s8[4194304]{0:T(1024)(128)(4,1)S(1)}, s32[]{:S(2)}) async-start(s8[12582912]{0:T(1024)(128)(4,1)} %bitcast.286), calls=%async_computation.10 | async-start | bytes 8388608
  106.4 3.6 copy-start.12
  128.7 2.5 copy-start.2
  133.4 47.6 %copy-start.17 = (bf16[384,256]{1,0:T(8,128)(2,1)S(1)}, bf16[384,256]{1,0:T(8,128)(2,1)}, u32[]{:S(2)}) copy-start(bf16[384,256]{1,0:T(8,128)(2,1)} %param.12) | copy-start | bytes 589828
  133.4 47.6 %copy-start.19 = (f32[256]{0:T(256)S(1)}, f32[256]{0:T(256)}, u32[]{:S(2)}) copy-start(f32[256]{0:T(256)} %param.11) | copy-start | bytes 3076
  151.2 58.8 %all-gather.5.cloned.1.call-start = ((), (), s32[]{:S(2)}) async-start(), calls=%async_computation.4 | async-start | bytes 1769472 | tf_op jit(solution)/shard_map/all_gather | solution.py:53
  183.0 302.3 %reduce-scatter.5.cloned.1.call-start = ((), (), s32[]{:S(2)}) async-start(), calls=%async_computation.5 | async-start | bytes 3342336 | tf_op jit(solution)/shard_map/reduce_scatter | solution.py:62
  210.1 4.2 copy-start.1
  210.1 18.3 %slice-start.3 = ((s8[12582912]{0:T(1024)(128)(4,1)}), s8[4194304]{0:T(1024)(128)(4,1)S(1)}, s32[]{:S(2)}) async-start(s8[12582912]{0:T(1024)(128)(4,1)} %bitcast.298), calls=%async_computation.11 | async-start | bytes 8388608
  214.2 14.1 %slice-start.4 = ((s8[12582912]{0:T(1024)(128)(4,1)}), s8[4194304]{0:T(1024)(128)(4,1)S(1)}, s32[]{:S(2)}) async-start(s8[12582912]{0:T(1024)(128)(4,1)} %bitcast.298), calls=%async_computation.12 | async-start | bytes 8388608
  221.2 7.1 %slice-start.5 = ((s8[12582912]{0:T(1024)(128)(4,1)}), s8[4194304]{0:T(1024)(128)(4,1)S(1)}, s32[]{:S(2)}) async-start(s8[12582912]{0:T(1024)(128)(4,1)} %bitcast.298), calls=%async_computation.13 | async-start | bytes 8388608
  410.9 74.3 %copy-start.16 = (bf16[384,256]{1,0:T(8,128)(2,1)S(1)}, bf16[384,256]{1,0:T(8,128)(2,1)}, u32[]{:S(2)}) copy-start(bf16[384,256]{1,0:T(8,128)(2,1)} %param.9) | copy-start | bytes 589828
  410.9 136.5 %all-reduce.3.cloned.1.call-start = ((), (), s32[]{:S(2)}) async-start(), calls=%async_computation.6 | async-start | bytes 524288 | tf_op jit(solution)/shard_map/psum | solution.py:76
  487.1 147.1 %all-reduce.5.cloned.1.call-start = ((), (), s32[]{:S(2)}) async-start(), calls=%async_computation.7 | async-start | bytes 524288 | tf_op jit(solution)/shard_map/psum | solution.py:76
  (9 other events, 21.3 us)
Sparse Core Ops, SparseCore 0:
  10.2 50.2 all-gather.2
  151.4 29.6 reduce-scatter.2
  183.3 26.6 all-gather.4
  411.1 74.1 reduce-scatter.4
  488.0 59.4 all-reduce.2
  550.5 83.7 all-reduce.4
